TPU v7x, 512 devices: a whole 4x8x8 slice. The times are simulated.
512 devices in a mesh: row: 16 (over y, core), col: 8 (over z), fib: 4 (over x).
Axes of the slice: x: 4, y: 8, z: 8, core: 2. Of those that a mesh axis runs over, the one named last changes fastest.
Arguments:
- values: bfloat16 [768, 12, 128, 128], P(('row', 'col'), 'fib'), may hold values from -3 to 3
- columns: int32 [768, 12], P(('row', 'col')), may hold values from 0 to 767, as said below
- counts: int32 [768], P(('row', 'col')), may hold values from 6 to 12, as said below
Outputs:
- square: bfloat16 [768, 12, 128, 128], P(('row', 'col'), 'fib')
- traces: float32 [2], replicated
Inputs may be any that keep to these rules, and one draw needn't show every extreme that they name: Slot 0 of block row i holds i. Every slot s >= 1 of row i, used or not, holds (i + o) mod 768 with 1 <= |o| <= 6, and the columns of one row are distinct. Row i uses slots 0 to counts[i] - 1; later slots are ignored. Some row uses all 12 slots.
All inputs are finite; a program needn't handle non-finite values.
Results may differ from a plain program's by a relative error of at most 0.001.
Values may be sent and summed in bfloat16 or wider, within the bound.
A program may use at most 128 MiB of HBM per device.

v0:
```python
import jax
import jax.numpy as jnp
from jax import lax
from jax.sharding import PartitionSpec as P

BAND = 6


def padded(array, sides, width):
    for axis, dim in sides:
        size, length = (lax.axis_size(axis), array.shape[dim])
        up = [(i, (i + 1) % size) for i in range(size)]
        down = [(j, i) for i, j in up]
        last = lax.slice_in_dim(array, length - width, length, axis=dim)
        initial = lax.slice_in_dim(array, 0, width, axis=dim)
        before = lax.ppermute(last, axis, up)
        after = lax.ppermute(initial, axis, down)
        array = jnp.concatenate([before, array, after], axis=dim)
    return array


def band_product(
    left_tiles, left_keep, fetch_index, target_cols, target_keep, window, window_cols, window_counts
):
    picked = jnp.take(window, fetch_index, axis=0)
    picked_cols = jnp.take(window_cols, fetch_index, axis=0)
    picked_counts = jnp.take(window_counts, fetch_index, axis=0)
    alive_slots = lax.broadcasted_iota(jnp.int32, picked_cols.shape, 1) < picked_counts[:, None]
    matches = (picked_cols[:, None, :] == target_cols[None, :, None]) & alive_slots[:, None, :]
    matches = matches & left_keep[:, None, None] & target_keep[None, :, None]
    chosen = jnp.einsum(
        "ajs,asxy->ajxy", matches.astype(jnp.bfloat16), picked, preferred_element_type=jnp.float32
    ).astype(jnp.bfloat16)
    return jnp.einsum("axy,ajyz->jxz", left_tiles, chosen, preferred_element_type=jnp.float32)


def body(values, columns, counts):
    rows_here = values.shape[0]
    share_count = values.shape[1]
    slot_count = columns.shape[1]
    block_total = rows_here * lax.axis_size(("row", "col"))
    fib_index = lax.axis_index("fib")
    full_rows = lax.all_gather(values, "fib", axis=1, tiled=True)
    window, window_cols, window_counts = (
        padded(full_rows, ((("row", "col"), 0),), BAND),
        padded(columns, ((("row", "col"), 0),), BAND),
        padded(counts, ((("row", "col"), 0),), BAND),
    )
    local_rows = jnp.arange(rows_here, dtype=jnp.int32)
    row_ids = lax.axis_index(("row", "col")) * rows_here + local_rows
    fetch_all = (columns - row_ids[:, None] + BAND) % block_total + local_rows[:, None]
    slot_ids = jnp.arange(slot_count, dtype=jnp.int32)
    keep_mask = slot_ids[None, :] < counts[:, None]
    first_slot = fib_index * share_count

    def one_row(operands):
        left_tiles, left_keep, fetch_index, target_cols, target_keep = operands
        return band_product(
            left_tiles,
            left_keep,
            fetch_index,
            target_cols,
            target_keep,
            window,
            window_cols,
            window_counts,
        )

    left_fetch = lax.dynamic_slice_in_dim(fetch_all, first_slot, share_count, 1)
    left_keep = lax.dynamic_slice_in_dim(keep_mask, first_slot, share_count, 1)
    partial_value = lax.map(one_row, (values, left_keep, left_fetch, columns, keep_mask))
    regrouped = lax.all_to_all(partial_value[None], "fib", split_axis=2, concat_axis=0, tiled=True)
    product = jnp.sum(regrouped, axis=0)
    is_first = (fib_index == 0).astype(jnp.float32)
    trace_values = is_first * jnp.sum(
        jnp.diagonal(values[:, 0].astype(jnp.float32), axis1=1, axis2=2)
    )
    trace_square = is_first * jnp.sum(jnp.diagonal(product[:, 0], axis1=1, axis2=2))
    traces = lax.psum(jnp.stack([trace_values, trace_square]), ("row", "col", "fib"))
    return (product.astype(jnp.bfloat16), traces)


def solution(mesh):
    in_specs = (P(("row", "col"), "fib", None, None), P(("row", "col"), None), P(("row", "col")))
    out_specs = (P(("row", "col"), "fib", None, None), P())
    return jax.shard_map(body, mesh=mesh, in_specs=in_specs, out_specs=out_specs, check_vma=False)
```

profile of v0, /device:TPU:1, one launch (start us, length us, event | category | flops | bytes accessed | tf_op | source)
XLA Modules:
  0.0 354.2 jit_solution(3832877042432415155)
XLA Ops:
  7.9 45.8 %all-gather.2.cloned.1.call-done = bf16[6,12,128,128]{3,2,1,0:T(8,128)(2,1)} async-done(((bf16[6,3,128,128]{3,2,1,0:T(8,128)(2,1)}), bf16[6,12,128,128]{3,2,1,0:T(8,128)(2,1)}) %all-gather.2.cloned.1.call-update) | async-done | bytes 2359312 | tf_op jit(solution)/shard_map/all_gather | solution.py:43
  53.7 3.3 collective-permute-start.4
  57.0 5.0 %collective-permute-start.5 = (bf16[6,12,128,128]{3,2,1,0:T(8,128)(2,1)}, bf16[6,12,128,128]{3,2,1,0:T(8,128)(2,1)}, u32[]{:S(2)}, u32[]{:S(2)}) collective-permute-start(bf16[6,12,128,128]{3,2,1,0:T(8,128)(2,1)} %all-gather.2.cloned.1.call-done), channel_id=1, source_target_pairs={{4,0},{8,4},{12,8},{16,12},{20,16},{24,20},{28,24},{32,28},{36,32}... | collective-permute-start | bytes 7077896 | tf_op jit(solution)/shard_map/ppermute | solution.py:17
  61.9 1.9 collective-permute-start
  63.8 4.9 %collective-permute-start.1 = (s32[6,12]{1,0:T(8,128)}, s32[6,12]{1,0:T(8,128)S(1)}, u32[]{:S(2)}, u32[]{:S(2)}) collective-permute-start(s32[6,12]{1,0:T(8,128)} %param.6), channel_id=1, source_target_pairs={{4,0},{8,4},{12,8},{16,12},{20,16},{24,20},{28,24},{32,28},{36,32}... | collective-permute-start | bytes 872 | tf_op jit(solution)/shard_map/ppermute | solution.py:17
  68.7 1.9 collective-permute-start.2
  70.7 0.7 iota_compare_fusion.1
  71.5 0.8 fusion.18
  72.3 39.8 %collective-permute-done.2 = s32[6]{0:T(128)S(1)} collective-permute-done((s32[6]{0:T(128)}, s32[6]{0:T(128)S(1)}, u32[]{:S(2)}, u32[]{:S(2)}) %collective-permute-start.2) | collective-permute-done | bytes 56 | tf_op jit(solution)/shard_map/ppermute | solution.py:16
  112.2 2.9 collective-permute-start.3
  115.1 1.5 collective-permute-done.3
  116.6 0.7 pad_add_fusion.1
  117.3 0.7 pad_add_fusion
  118.1 5.9 %pad_maximum_fusion = bf16[18,12,128,128]{3,2,1,0:T(8,128)(2,1)} fusion(bf16[6,12,128,128]{3,2,1,0:T(8,128)(2,1)} %collective-permute-done.5, bf16[6,12,128,128]{3,2,1,0:T(8,128)(2,1)} %all-gather.2.cloned.1.call-done, bf16[6,12,128,128]{3,2,1,0:T(8,128)(2,1)S(1)} %collective-permute-done.4), kind=kLoop, calls=%fused_computation.37 | loop fusion | flops 7077888 | bytes 14155776 | tf_op jit(solution)/shard_map/concatenate | solution.py:18
  123.9 50.9 %while.10 = (s32[]{:T(128)}, f32[6,12,128,128]{2,3,0,1:T(8,128)}, s32[6,3]{1,0:T(8,128)S(1)}, s32[18,12]{1,0:T(8,128)S(1)}, s32[6,12]{1,0:T(8,128)}, /*index=5*/...) while((s32[]{:T(128)}, f32[6,12,128,128]{2,3,0,1:T(8,128)}, ...), condition=%wide.region_1.2_spmd, body=%wide.region_0.1_spmd.sunk | while | flops 166333216 | bytes 9541871 | solution.py:71
  124.6 3.8 %gather_fusion = bf16[3,12,128,128]{3,2,1,0:T(8,128)(2,1)S(1)} fusion(bf16[18,12,128,128]{3,2,1,0:T(8,128)(2,1)} %get-tuple-element.178, s32[1024]{0:T(1024)S(1)} %pad_clamp_fusion.2), kind=kCustom, calls=%fused_computation.2.clone.1 | custom fusion | bytes 2359308 | tf_op jit(solution)/shard_map/while/body/eval_jaxpr/jit(_take)/gather | solution.py:25
  130.0 0.9 convolution_convert_fusion.2
  131.0 1.5 fusion.32
  133.1 3.8 %gather_fusion = bf16[3,12,128,128]{3,2,1,0:T(8,128)(2,1)S(1)} fusion(bf16[18,12,128,128]{3,2,1,0:T(8,128)(2,1)} %get-tuple-element.178, s32[1024]{0:T(1024)S(1)} %pad_clamp_fusion.2), kind=kCustom, calls=%fused_computation.2.clone.1 | custom fusion | bytes 2359308 | tf_op jit(solution)/shard_map/while/body/eval_jaxpr/jit(_take)/gather | solution.py:25
  137.8 0.7 fusion.31
  138.5 0.9 convolution_convert_fusion.2
  139.4 1.5 fusion.32
  141.6 3.8 %gather_fusion = bf16[3,12,128,128]{3,2,1,0:T(8,128)(2,1)S(1)} fusion(bf16[18,12,128,128]{3,2,1,0:T(8,128)(2,1)} %get-tuple-element.178, s32[1024]{0:T(1024)S(1)} %pad_clamp_fusion.2), kind=kCustom, calls=%fused_computation.2.clone.1 | custom fusion | bytes 2359308 | tf_op jit(solution)/shard_map/while/body/eval_jaxpr/jit(_take)/gather | solution.py:25
  146.3 0.7 fusion.31
  147.0 0.9 convolution_convert_fusion.2
  147.9 1.5 fusion.32
  150.1 3.8 %gather_fusion = bf16[3,12,128,128]{3,2,1,0:T(8,128)(2,1)S(1)} fusion(bf16[18,12,128,128]{3,2,1,0:T(8,128)(2,1)} %get-tuple-element.178, s32[1024]{0:T(1024)S(1)} %pad_clamp_fusion.2), kind=kCustom, calls=%fused_computation.2.clone.1 | custom fusion | bytes 2359308 | tf_op jit(solution)/shard_map/while/body/eval_jaxpr/jit(_take)/gather | solution.py:25
  154.8 0.7 fusion.31
  155.5 0.9 convolution_convert_fusion.2
  156.4 1.5 fusion.32
  158.5 3.8 %gather_fusion = bf16[3,12,128,128]{3,2,1,0:T(8,128)(2,1)S(1)} fusion(bf16[18,12,128,128]{3,2,1,0:T(8,128)(2,1)} %get-tuple-element.178, s32[1024]{0:T(1024)S(1)} %pad_clamp_fusion.2), kind=kCustom, calls=%fused_computation.2.clone.1 | custom fusion | bytes 2359308 | tf_op jit(solution)/shard_map/while/body/eval_jaxpr/jit(_take)/gather | solution.py:25
  163.2 0.7 fusion.31
  163.9 0.9 convolution_convert_fusion.2
  164.9 1.5 fusion.32
  167.0 3.8 %gather_fusion = bf16[3,12,128,128]{3,2,1,0:T(8,128)(2,1)S(1)} fusion(bf16[18,12,128,128]{3,2,1,0:T(8,128)(2,1)} %get-tuple-element.178, s32[1024]{0:T(1024)S(1)} %pad_clamp_fusion.2), kind=kCustom, calls=%fused_computation.2.clone.1 | custom fusion | bytes 2359308 | tf_op jit(solution)/shard_map/while/body/eval_jaxpr/jit(_take)/gather | solution.py:25
  171.7 0.7 fusion.31
  172.4 0.9 convolution_convert_fusion.2
  173.3 1.5 fusion.32
  174.8 5.0 %all-to-all-start = ((f32[1,6,12,128,128]{3,4,1,0,2:T(8,128)}), f32[1,6,12,128,128]{3,4,1,0,2:T(8,128)}, u32[]{:S(2)}, u32[]{:S(2)}) async-start(f32[1,6,12,128,128]{3,4,1,0,2:T(8,128)} %bitcast.60), calls=%async_computation | async-start | bytes 9437184 | tf_op jit(solution)/shard_map/all_to_all | solution.py:72
  179.9 3.3 copy.13
  183.2 6.5 %bitcast_convert_fusion = f32[6,128,128]{0,2,1:T(8,128)} fusion(bf16[6,1,128,128]{0,3,2,1:T(8,128)(2,1)} %copy.13), kind=kLoop, calls=%fused_computation.38 | loop fusion | flops 98304 | bytes 589824 | tf_op jit(solution)/shard_map/convert_element_type | solution.py:76
  189.7 1.8 gather_fusion.3
  192.7 40.7 %all-to-all-done = f32[1,6,12,128,128]{3,4,1,0,2:T(8,128)} async-done(((f32[1,6,12,128,128]{3,4,1,0,2:T(8,128)}), f32[1,6,12,128,128]{3,4,1,0,2:T(8,128)}, u32[]{:S(2)}, u32[]{:S(2)}) %all-to-all-start) | async-done | bytes 4718624 | tf_op jit(solution)/shard_map/all_to_all | solution.py:72
  233.4 2.9 reduce_sum.27
  236.4 7.6 %copy.21 = f32[6,1,128,128]{0,3,2,1:T(8,128)} copy(f32[6,1,128,128]{2,3,1,0:T(8,128)S(1)} %copy.33) | data formatting | bytes 786432
  244.0 1.8 gather_fusion.4
  247.2 99.0 %psum.7 = f32[2]{0:T(128)} all-reduce(f32[2]{0:T(128)S(1)} %pad_maximum_fusion.1), channel_id=1, replica_groups=mesh['row'=16,'col'=8,'fib'=4] {'row','col','fib'}, use_global_device_ids=true, to_apply=%region_5.6 | all-reduce | flops 2 | bytes 16 | tf_op jit(solution)/shard_map/psum | solution.py:79
  346.3 1.1 copy.15
  (81 shorter events, 12.5 us)
Async XLA Ops:
  7.2 46.5 %all-gather.2.cloned.1.call-start = ((), (), s32[]{:S(2)}) async-start(), calls=%async_computation.1 | async-start | bytes 2949120 | tf_op jit(solution)/shard_map/all_gather | solution.py:43
  53.7 64.4 %collective-permute-start.4 = (bf16[6,12,128,128]{3,2,1,0:T(8,128)(2,1)}, bf16[6,12,128,128]{3,2,1,0:T(8,128)(2,1)S(1)}, u32[]{:S(2)}, u32[]{:S(2)}) collective-permute-start(bf16[6,12,128,128]{3,2,1,0:T(8,128)(2,1)} %all-gather.2.cloned.1.call-done), channel_id=1, source_target_pairs={{0,4},{4,8},{8,12},{12,16},{16,20},{20,24},{24,28},{28,32},{32,36}... | collective-permute-start | bytes 7077896 | tf_op jit(solution)/shard_map/ppermute | solution.py:16
  57.0 61.1 %collective-permute-start.5 = (bf16[6,12,128,128]{3,2,1,0:T(8,128)(2,1)}, bf16[6,12,128,128]{3,2,1,0:T(8,128)(2,1)}, u32[]{:S(2)}, u32[]{:S(2)}) collective-permute-start(bf16[6,12,128,128]{3,2,1,0:T(8,128)(2,1)} %all-gather.2.cloned.1.call-done), channel_id=1, source_target_pairs={{4,0},{8,4},{12,8},{16,12},{20,16},{24,20},{28,24},{32,28},{36,32}... | collective-permute-start | bytes 7077896 | tf_op jit(solution)/shard_map/ppermute | solution.py:17
  61.9 55.4 %collective-permute-start = (s32[6,12]{1,0:T(8,128)}, s32[6,12]{1,0:T(8,128)S(1)}, u32[]{:S(2)}, u32[]{:S(2)}) collective-permute-start(s32[6,12]{1,0:T(8,128)} %param.6), channel_id=1, source_target_pairs={{0,4},{4,8},{8,12},{12,16},{16,20},{20,24},{24,28},{28,32},{32,36}... | collective-permute-start | bytes 872 | tf_op jit(solution)/shard_map/ppermute | solution.py:16
  63.8 53.5 %collective-permute-start.1 = (s32[6,12]{1,0:T(8,128)}, s32[6,12]{1,0:T(8,128)S(1)}, u32[]{:S(2)}, u32[]{:S(2)}) collective-permute-start(s32[6,12]{1,0:T(8,128)} %param.6), channel_id=1, source_target_pairs={{4,0},{8,4},{12,8},{16,12},{20,16},{24,20},{28,24},{32,28},{36,32}... | collective-permute-start | bytes 872 | tf_op jit(solution)/shard_map/ppermute | solution.py:17
  68.7 43.5 %collective-permute-start.2 = (s32[6]{0:T(128)}, s32[6]{0:T(128)S(1)}, u32[]{:S(2)}, u32[]{:S(2)}) collective-permute-start(s32[6]{0:T(128)} %param.7), channel_id=1, source_target_pairs={{0,4},{4,8},{8,12},{12,16},{16,20},{20,24},{24,28},{28,32},{32,36}... | collective-permute-start | bytes 80 | tf_op jit(solution)/shard_map/ppermute | solution.py:16
  112.2 4.4 %collective-permute-start.3 = (s32[6]{0:T(128)}, s32[6]{0:T(128)S(1)}, u32[]{:S(2)}, u32[]{:S(2)}) collective-permute-start(s32[6]{0:T(128)} %param.7), channel_id=1, source_target_pairs={{4,0},{8,4},{12,8},{16,12},{20,16},{24,20},{28,24},{32,28},{36,32}... | collective-permute-start | bytes 80 | tf_op jit(solution)/shard_map/ppermute | solution.py:17
  118.0 5.9 %copy-start = (bf16[6,3,128,128]{3,2,1,0:T(8,128)(2,1)S(1)}, bf16[6,3,128,128]{3,2,1,0:T(8,128)(2,1)}, u32[]{:S(2)}) copy-start(bf16[6,3,128,128]{3,2,1,0:T(8,128)(2,1)} %param.5) | copy-start | bytes 1769476
  174.8 58.6 %all-to-all-start = ((f32[1,6,12,128,128]{3,4,1,0,2:T(8,128)}), f32[1,6,12,128,128]{3,4,1,0,2:T(8,128)}, u32[]{:S(2)}, u32[]{:S(2)}) async-start(f32[1,6,12,128,128]{3,4,1,0,2:T(8,128)} %bitcast.60), calls=%async_computation | async-start | bytes 9437184 | tf_op jit(solution)/shard_map/all_to_all | solution.py:72
Sparse Core Ops, SparseCore 0:
  10.1 43.5 all-gather.1
where the time goes:
time: 355 us; the launch traced here: 354 us
  waiting for transfers between devices  129 us (36%)
  blocking collectives  99 us (28%)
  local copies, waits for them, and re-layouts  50 us (14%)
  starting transfers between devices  24.9 us (7%)
  other arithmetic  21.6 us (6%)
  between operations  15.5 us (4%)
  matrix products  14.4 us (4%)
    psum x1, blocking collectives, body(): lax.psum(jnp.stack([trace_values, trace_square]), ('row', 'col', 'fib'))  99 us
    all_gather x1, waiting for transfers between devices, body(): full_rows = lax.all_gather(values, 'fib', axis=1, tiled=True)  45.8 us
    all_to_all x1, waiting for transfers between devices, body(): lax.all_to_all(partial_value[None], 'fib', split_axis=2, concat_axis=0, t...  40.7 us
    ppermute x3, waiting for transfers between devices, padded(): before = lax.ppermute(last, axis, up)  39.8 us
    gather x6, local copies, waits for them, and re-layouts, band_product(): picked = jnp.take(window, fetch_index, axis=0)  22.7 us
    ppermute x3, starting transfers between devices, padded(): after = lax.ppermute(initial, axis, down)  12.7 us
    dot_general x6, matrix products, band_product(): jnp.einsum('axy,ajyz->jxz', left_tiles, chosen, preferred_element_type=jn...  8.83 us
    unnamed x6, local copies, waits for them, and re-layouts  8.81 us
  transfers between devices with their start and end apart: 8, of which 4 were waited for; matrix products, arithmetic and copies ran while one was open for 4% of the time, Pallas kernels for 0%

commit v1 on v0

v1 whole, which is shorter than its diff:
```python
import functools

import jax
import jax.numpy as jnp
from jax import lax
from jax.experimental import pallas as pl
from jax.experimental.pallas import tpu as pltpu
from jax.sharding import PartitionSpec as P

MESH = pl.DeviceIdType.MESH
BAND = 6
R = 6
T = 3
S = 12
NO = 2 * BAND + 1
B = 128
QB = 32


def kernel(sizes, v_ref, col_ref, cnt_ref, out_ref, tr_ref, L, Q, acc, send, land, tab, ntab, tx, tz, ty,
           stab, sprev, snext, own_s, own_r, rel_s, rel_r, z_s, z_r, tab_s, tab_r, loc, out_s, out_r,
           tx_s, tx_r, tz_s, tz_r, ty_s, ty_r, *halo):
    n_row, n_col, n_fib = sizes
    n_blocks = n_row * n_col * R
    row, col, fib = (lax.axis_index(a) for a in ("row", "col", "fib"))
    group = row * n_col + col

    def along_fib(d):
        return (row, col, lax.rem(fib + d + n_fib, n_fib))

    def along_col(d):
        return (row, lax.rem(col + d, n_col), fib)

    def along_row(d):
        return (lax.rem(row + d, n_row), col, fib)

    def along_group(d):
        other = lax.rem(group + d + n_row * n_col, n_row * n_col)
        return (other // n_col, lax.rem(other, n_col), fib)

    peers = [along_fib(d) for d in range(1, n_fib)] + [along_group(1), along_group(-1)]
    peers += [along_col(d) for d in range(1, n_col)] + [along_row(d) for d in range(1, n_row)]
    barrier = pltpu.get_barrier_semaphore()
    for peer in peers:
        pl.semaphore_signal(barrier, inc=1, device_id=peer, device_id_type=MESH)

    def remote(src, dst, ssem, rsem, device):
        return pltpu.make_async_remote_copy(
            src_ref=src, dst_ref=dst, send_sem=ssem, recv_sem=rsem, device_id=device, device_id_type=MESH
        )

    mine = pl.multiple_of(fib * QB, QB)
    quarter = pl.ds(mine, QB)
    prev, nxt = halo[:R], halo[R:]

    def flip(r, _):
        for t in range(T):
            L[r, T * fib + t] = v_ref[r, t].T
        L[r, S] = jnp.zeros((B, B), jnp.bfloat16)
        return 0

    lax.fori_loop(0, R, flip, 0)
    for ref in halo:
        ref[S] = jnp.zeros((QB, B), jnp.bfloat16)

    rows = lax.broadcasted_iota(jnp.int32, (8, B), 0)
    lanes = lax.broadcasted_iota(jnp.int32, (8, B), 1)
    table, place = jnp.full((8, B), S, jnp.int32), jnp.full((8, B), NO, jnp.int32)
    columns = jnp.concatenate([col_ref[...], jnp.zeros((8 - R, S), jnp.int32)], axis=0)
    counts = jnp.zeros((8, B), jnp.int32)
    for r in range(R):
        counts = jnp.where(rows == r, cnt_ref[r], counts)
    for s in range(S):
        offset = columns[:, s : s + 1] - (group * R + rows) + BAND
        offset = jnp.where(offset < 0, offset + n_blocks, offset)
        offset = jnp.where(offset >= n_blocks, offset - n_blocks, offset)
        table = jnp.where((offset == lanes) & (s < counts), s, table)
        place = jnp.where((lanes == s) & (s < counts), offset, place)
    tab[0:8, :] = table
    tab[8:16, :] = place

    def clear(w, _):
        Q[w, 0:BAND] = jnp.zeros((BAND, QB, B), jnp.bfloat16)
        Q[w, BAND + NO : 2 * BAND + NO] = jnp.zeros((BAND, QB, B), jnp.bfloat16)
        return 0

    lax.fori_loop(0, 3 * R, clear, 0)
    for r in range(R):
        acc[r, NO] = jnp.zeros((QB, B), jnp.float32)

    local = pltpu.make_async_copy(tab, stab, loc.at[0])
    local.start()
    local.wait()
    pl.semaphore_wait(barrier, len(peers))

    def own(r, way):
        part = L.at[r, pl.ds(T * fib, T)]
        return remote(part, part, own_s.at[way, r], own_r.at[way, r], along_fib(1 - 2 * way))

    def relay(r, way):
        cut = 2 - r % 2
        source = lax.rem(fib + (n_fib - 1 if way == 0 else 1), n_fib)
        part = L.at[r, pl.ds(T * source, cut)] if way == 0 else L.at[r, pl.ds(T * source + cut, T - cut)]
        return remote(part, part, rel_s.at[way, r], rel_r.at[way, r], along_fib(1 - 2 * way))

    def shift(r, way):
        dst = (prev if way == 0 else nxt)[r].at[0:S]
        return remote(L.at[r, 0:S, quarter], dst, z_s.at[way, r], z_r.at[way, r], along_group(1 - 2 * way))

    def tables(way):
        return remote(tab.at[0:8], ntab.at[way], tab_s.at[way], tab_r.at[way], along_group(1 - 2 * way))

    for r in range(2):
        own(r, 0).start()
        own(r, 1).start()
    tables(0).start()
    tables(1).start()
    for r in range(R):
        own(r, 0).wait_recv()
        own(r, 1).wait_recv()
        relay(r, 0).start()
        relay(r, 1).start()
        if r + 2 < R:
            own(r + 2, 0).start()
            own(r + 2, 1).start()
        if r >= 1:
            relay(r - 1, 0).wait_recv()
            relay(r - 1, 1).wait_recv()
            shift(r - 1, 0).start()
            shift(r - 1, 1).start()
    relay(R - 1, 0).wait_recv()
    relay(R - 1, 1).wait_recv()
    shift(R - 1, 0).start()
    shift(R - 1, 1).start()

    tables(0).wait_recv()
    tables(1).wait_recv()
    near = (pltpu.make_async_copy(ntab.at[0], sprev, loc.at[1]), pltpu.make_async_copy(ntab.at[1], snext, loc.at[2]))
    for copy in near:
        copy.start()

    def place_own(r, _):
        for o in range(NO):
            Q[R + r, BAND + o] = L[r, stab[r, o], quarter]
        return 0

    lax.fori_loop(0, R, place_own, 0)

    def term(i, w):
        return Q[w, pl.ds(BAND + R + i - w, NO)].reshape(NO * QB, B), L[i, stab[i, w - i]]

    def products(i, window):
        pairs = [term(i, w) for w in window]
        right = jnp.concatenate([p[0] for p in pairs], axis=1)
        left = jnp.concatenate([p[1] for p in pairs], axis=0)
        return jnp.dot(right, left, preferred_element_type=jnp.float32).reshape(NO, QB, B)

    def own_part(i, _):
        acc[i, 0:NO] = products(i, range(R, 2 * R))
        return 0

    lax.fori_loop(0, R, own_part, 0)
    for copy in near:
        copy.wait()
    for r in range(R):
        shift(r, 0).wait_recv()
        shift(r, 1).wait_recv()
        for o in range(NO):
            Q[r, BAND + o] = prev[r][sprev[r, o]]
            Q[2 * R + r, BAND + o] = nxt[r][snext[r, o]]

    def deliver(i, d):
        dst = land.at[i, :, quarter]
        return remote(send.at[d - 1, i], dst, out_s.at[d - 1, i], out_r.at[d - 1, i], along_fib(d))

    diagonal = lax.broadcasted_iota(jnp.int32, (QB, B), 1) == lax.broadcasted_iota(jnp.int32, (QB, B), 0) + mine
    trace_values = jnp.zeros((QB, B), jnp.float32)
    trace_square = jnp.zeros((QB, B), jnp.float32)
    for i in range(R):
        acc[i, 0:NO] += products(i, [*range(i, R), *range(2 * R, 2 * R + i + 1)])
        trace_values += L[i, 0, quarter].astype(jnp.float32)
        trace_square += acc[i, BAND]
        for d in range(n_fib):
            owner = lax.rem(fib + d, n_fib)
            for t in range(T):
                block = acc[i, stab[8 + i, T * owner + t]].astype(jnp.bfloat16)
                if d == 0:
                    land[i, t, quarter] = block
                else:
                    send[d - 1, i, t] = block
        if i >= 1:
            for d in range(1, n_fib):
                deliver(i - 1, d).start()

    def total(tile):
        return jnp.sum(jnp.where(diagonal, tile, 0.0), axis=0, keepdims=True)

    first = jnp.where(rows == 0, total(trace_values), jnp.where(rows == 1, total(trace_square), 0.0))
    tx[fib] = first
    for d in range(1, n_fib):
        deliver(R - 1, d).start()

    def spread(buf, me, size, ssem, rsem, device):
        return [remote(buf.at[me], buf.at[me], ssem.at[d - 1], rsem.at[d - 1], device(d)) for d in range(1, size)]

    def add(buf, size):
        tile = buf[0]
        for k in range(1, size):
            tile += buf[k]
        return tile

    def finish(i):
        for d in range(1, n_fib):
            deliver(i, d).wait_recv()
        for t in range(T):
            out_ref[i, t] = land[i, t].T

    stage_x = spread(tx, fib, n_fib, tx_s, tx_r, along_fib)
    stage_z = spread(tz, col, n_col, tz_s, tz_r, along_col)
    stage_y = spread(ty, row, n_row, ty_s, ty_r, along_row)
    for copy in stage_x:
        copy.start()
    for copy in stage_x:
        copy.wait_recv()
    tz[col] = add(tx, n_fib)
    for copy in stage_z:
        copy.start()
    for copy in stage_z:
        copy.wait_recv()
    ty[row] = add(tz, n_col)
    for copy in stage_y:
        copy.start()
    for i in range(R):
        finish(i)
    for copy in stage_y:
        copy.wait_recv()
    sums = add(ty, n_row)
    tr_ref[0] = jnp.sum(sums[0:1])
    tr_ref[1] = jnp.sum(sums[1:2])

    for copy in [*stage_x, *stage_y, *stage_z, tables(0), tables(1)]:
        copy.wait_send()
    for r in range(R):
        for way in range(2):
            own(r, way).wait_send()
            relay(r, way).wait_send()
            shift(r, way).wait_send()
        for d in range(1, n_fib):
            deliver(r, d).wait_send()


def solution(mesh):
    sizes = tuple(mesh.shape[a] for a in ("row", "col", "fib"))
    bf16, f32, i32 = jnp.bfloat16, jnp.float32, jnp.int32
    dma = pltpu.SemaphoreType.DMA

    def body(values, columns, counts):
        vmem, smem = pl.BlockSpec(memory_space=pltpu.VMEM), pl.BlockSpec(memory_space=pltpu.SMEM)
        return pl.pallas_call(
            functools.partial(kernel, sizes),
            out_shape=(jax.ShapeDtypeStruct((R, T, B, B), bf16), jax.ShapeDtypeStruct((2,), f32)),
            in_specs=[vmem, vmem, smem],
            out_specs=(vmem, smem),
            scratch_shapes=[
                pltpu.VMEM((R, S + 1, B, B), bf16),
                pltpu.VMEM((3 * R, NO + 2 * BAND, QB, B), bf16),
                pltpu.VMEM((R, NO + 1, QB, B), f32),
                pltpu.VMEM((3, R, T, QB, B), bf16),
                pltpu.VMEM((R, T, B, B), bf16),
                pltpu.VMEM((16, B), i32),
                pltpu.VMEM((2, 8, B), i32),
                *(pltpu.VMEM((n, 8, B), f32) for n in (sizes[2], sizes[1], sizes[0])),
                pltpu.SMEM((16, B), i32),
                pltpu.SMEM((8, B), i32),
                pltpu.SMEM((8, B), i32),
                *[dma((2, R))] * 6,
                dma((2,)),
                dma((2,)),
                dma((3,)),
                dma((3, R)),
                dma((3, R)),
                *(dma((n - 1,)) for n in (sizes[2], sizes[2], sizes[1], sizes[1], sizes[0], sizes[0])),
                *[pltpu.VMEM((S + 1, QB, B), bf16)] * (2 * R),
            ],
            compiler_params=pltpu.CompilerParams(collective_id=0, has_side_effects=True),
        )(values, columns, counts)

    in_specs = (P(("row", "col"), "fib", None, None), P(("row", "col"), None), P(("row", "col")))
    out_specs = (P(("row", "col"), "fib", None, None), P())
    return jax.shard_map(body, mesh=mesh, in_specs=in_specs, out_specs=out_specs, check_vma=False)
```

time: 355 us -> 67.7 us (0.19)
  waiting for transfers between devices: 129 us -> 0 us
  blocking collectives: 99 us -> 0 us
  Pallas kernels: 0 us -> 64.5 us
  local copies, waits for them, and re-layouts: 50 us -> 2.45 us
  starting transfers between devices: 24.9 us -> 0 us
  other arithmetic: 21.6 us -> 0 us
  between operations: 15.5 us -> 0.65 us
  matrix products: 14.4 us -> 0 us
    psum x1 -> x0, blocking collectives: 99 us -> none  [body(): lax.psum(jnp.stack([trace_values, trace_square]), ('row', 'col', 'fib'))]
    pallas_call x0 -> x1, Pallas kernels: none -> 64.5 us  [body(): pl.pallas_call(functools.partial(kernel, sizes), out_shape=(jax.ShapeDtyp...]
    all_gather x1 -> x0, waiting for transfers between devices: 45.8 us -> none  [body(): full_rows = lax.all_gather(values, 'fib', axis=1, tiled=True)]
    ppermute x6 -> x0, waiting for transfers between devices: 41.4 us -> none  [the longest x3 39.8 us: padded(): before = lax.ppermute(last, axis, up)]
    all_to_all x1 -> x0, waiting for transfers between devices: 40.7 us -> none  [body(): lax.all_to_all(partial_value[None], 'fib', split_axis=2, concat_axis=0, t...]
    gather x20 -> x0, local copies, waits for them, and re-layouts: 33.4 us -> none  [the longest x6 22.7 us: band_product(): picked = jnp.take(window, fetch_index, axis=0)]
    ppermute x6 -> x0, starting transfers between devices: 19.8 us -> none  [the longest x3 12.7 us: padded(): after = lax.ppermute(initial, axis, down)]
    dot_general x12 -> x0, matrix products: 14.4 us -> none  [the longest x6 8.83 us: band_product(): jnp.einsum('axy,ajyz->jxz', left_tiles, chosen, preferred_element_type=jn...]
  transfers between devices with their start and end apart: 8 -> 0, of which waited for: 4 -> 0; matrix products, arithmetic and copies ran while one was open for 4% -> 0% of each run, Pallas kernels for 0% -> 0%
where the time goes in v1:
time: 67.7 us; the launch traced here: 67.6 us
  Pallas kernels  64.5 us (95%)
  local copies, waits for them, and re-layouts  2.45 us (4%)
    pallas_call x1, Pallas kernels, body(): pl.pallas_call(functools.partial(kernel, sizes), out_shape=(jax.ShapeDtyp...  64.5 us
    unnamed x4, local copies, waits for them, and re-layouts  2.45 us

profile of v1, /device:TPU:1, one launch (start us, length us, event | category | flops | bytes accessed | tf_op | source)
XLA Modules:
  0.0 67.6 jit_solution(7387747893986889531)
XLA Ops:
  0.6 64.5 %shard_map.50 = (bf16[6,3,128,128]{3,2,1,0:T(8,128)(2,1)}, f32[2]{0:T(128)}) custom-call(bf16[6,3,128,128]{3,2,1,0:T(8,128)(2,1)} %v_ref.1, s32[6,12]{1,0:T(8,128)} %col_ref.1, s32[6]{0:T(128)} %cnt_ref.1), custom_call_target="tpu_custom_call" | custom-call | tf_op jit(solution)/shard_map/pallas_call | solution.py:259
  65.1 0.0 copy-start
  65.1 1.9 %copy.7 = bf16[6,3,128,128]{3,2,1,0:T(8,128)(2,1)} copy(bf16[6,3,128,128]{3,2,1,0:T(8,128)(2,1)} %get-tuple-element.4) | data formatting | bytes 1179648
  67.1 0.0 copy-done
  67.1 0.5 copy.8
Async XLA Ops:
  65.1 1.9 %copy-start = (f32[2]{0:T(128)S(1)}, f32[2]{0:T(128)}, u32[]{:S(2)}) copy-start(f32[2]{0:T(128)} %get-tuple-element.5) | copy-start | bytes 28

commit v2 on v1

--- a/solution.py
+++ b/solution.py
@@ -17,7 +17,7 @@
 QB = 32
 
 
-def kernel(sizes, v_ref, col_ref, cnt_ref, out_ref, tr_ref, L, Q, acc, send, land, tab, ntab, tx, tz, ty,
+def kernel(sizes, v_ref, col_ref, cnt_ref, out_ref, tr_ref, held, held_s, L, Q, acc, send, land, tab, ntab, tx, tz, ty,
            stab, sprev, snext, own_s, own_r, rel_s, rel_r, z_s, z_r, tab_s, tab_r, loc, out_s, out_r,
            tx_s, tx_r, tz_s, tz_r, ty_s, ty_r, *halo):
     n_row, n_col, n_fib = sizes
@@ -53,15 +53,44 @@
     quarter = pl.ds(mine, QB)
     prev, nxt = halo[:R], halo[R:]
 
-    def flip(r, _):
+    fetches = [pltpu.make_async_copy(v_ref.at[r], held.at[r], held_s.at[r]) for r in range(R)]
+    for fetch in fetches:
+        fetch.start()
+
+    def flip(r):
+        fetches[r].wait()
         for t in range(T):
-            L[r, T * fib + t] = v_ref[r, t].T
-        L[r, S] = jnp.zeros((B, B), jnp.bfloat16)
-        return 0
-
-    lax.fori_loop(0, R, flip, 0)
-    for ref in halo:
-        ref[S] = jnp.zeros((QB, B), jnp.bfloat16)
+            L[r, T * fib + t] = held[r, t].T
+
+    def own(r, way):
+        part = L.at[r, pl.ds(T * fib, T)]
+        return remote(part, part, own_s.at[way, r], own_r.at[way, r], along_fib(1 - 2 * way))
+
+    def relay(r, way):
+        cut = 2 - r % 2
+        source = lax.rem(fib + (n_fib - 1 if way == 0 else 1), n_fib)
+        part = L.at[r, pl.ds(T * source, cut)] if way == 0 else L.at[r, pl.ds(T * source + cut, T - cut)]
+        return remote(part, part, rel_s.at[way, r], rel_r.at[way, r], along_fib(1 - 2 * way))
+
+    def shift(r, way, d):
+        part = pl.ds(T * lax.rem(fib + d, n_fib), T)
+        dst = (prev if way == 0 else nxt)[r].at[part]
+        return remote(L.at[r, part, quarter], dst, z_s.at[way, r, d], z_r.at[way, r, d], along_group(1 - 2 * way))
+
+    def both(make, *where):
+        make(*where[:1], 0, *where[1:]).start()
+        make(*where[:1], 1, *where[1:]).start()
+
+    def tables(way):
+        return remote(tab.at[0:8], ntab.at[way], tab_s.at[way], tab_r.at[way], along_group(1 - 2 * way))
+
+    flip(0)
+    flip(1)
+    pl.semaphore_wait(barrier, len(peers))
+    both(own, 0)
+    both(own, 1)
+    for r in range(2, R):
+        flip(r)
 
     rows = lax.broadcasted_iota(jnp.int32, (8, B), 0)
     lanes = lax.broadcasted_iota(jnp.int32, (8, B), 1)
@@ -85,54 +114,35 @@
         return 0
 
     lax.fori_loop(0, 3 * R, clear, 0)
+    for ref in halo:
+        ref[S] = jnp.zeros((QB, B), jnp.bfloat16)
     for r in range(R):
         acc[r, NO] = jnp.zeros((QB, B), jnp.float32)
+        L[r, S] = jnp.zeros((B, B), jnp.bfloat16)
 
     local = pltpu.make_async_copy(tab, stab, loc.at[0])
     local.start()
-    local.wait()
-    pl.semaphore_wait(barrier, len(peers))
-
-    def own(r, way):
-        part = L.at[r, pl.ds(T * fib, T)]
-        return remote(part, part, own_s.at[way, r], own_r.at[way, r], along_fib(1 - 2 * way))
-
-    def relay(r, way):
-        cut = 2 - r % 2
-        source = lax.rem(fib + (n_fib - 1 if way == 0 else 1), n_fib)
-        part = L.at[r, pl.ds(T * source, cut)] if way == 0 else L.at[r, pl.ds(T * source + cut, T - cut)]
-        return remote(part, part, rel_s.at[way, r], rel_r.at[way, r], along_fib(1 - 2 * way))
-
-    def shift(r, way):
-        dst = (prev if way == 0 else nxt)[r].at[0:S]
-        return remote(L.at[r, 0:S, quarter], dst, z_s.at[way, r], z_r.at[way, r], along_group(1 - 2 * way))
-
-    def tables(way):
-        return remote(tab.at[0:8], ntab.at[way], tab_s.at[way], tab_r.at[way], along_group(1 - 2 * way))
-
-    for r in range(2):
-        own(r, 0).start()
-        own(r, 1).start()
+    for r in range(R):
+        both(shift, r, 0)
     tables(0).start()
     tables(1).start()
     for r in range(R):
         own(r, 0).wait_recv()
         own(r, 1).wait_recv()
-        relay(r, 0).start()
-        relay(r, 1).start()
+        both(relay, r)
         if r + 2 < R:
-            own(r + 2, 0).start()
-            own(r + 2, 1).start()
+            both(own, r + 2)
+        both(shift, r, 1)
+        both(shift, r, n_fib - 1)
         if r >= 1:
             relay(r - 1, 0).wait_recv()
             relay(r - 1, 1).wait_recv()
-            shift(r - 1, 0).start()
-            shift(r - 1, 1).start()
+            both(shift, r - 1, 2)
     relay(R - 1, 0).wait_recv()
     relay(R - 1, 1).wait_recv()
-    shift(R - 1, 0).start()
-    shift(R - 1, 1).start()
-
+    both(shift, R - 1, 2)
+
+    local.wait()
     tables(0).wait_recv()
     tables(1).wait_recv()
     near = (pltpu.make_async_copy(ntab.at[0], sprev, loc.at[1]), pltpu.make_async_copy(ntab.at[1], snext, loc.at[2]))
@@ -162,12 +172,21 @@
     lax.fori_loop(0, R, own_part, 0)
     for copy in near:
         copy.wait()
-    for r in range(R):
-        shift(r, 0).wait_recv()
-        shift(r, 1).wait_recv()
+    def take(r):
+        for way in range(2):
+            for d in range(n_fib):
+                shift(r, way, d).wait_recv()
         for o in range(NO):
             Q[r, BAND + o] = prev[r][sprev[r, o]]
             Q[2 * R + r, BAND + o] = nxt[r][snext[r, o]]
+
+    for r in range(R - 1):
+        take(r)
+    for i in range(R):
+        acc[i, 0:NO] += products(i, [*range(i, R - 1), *range(2 * R, 2 * R + min(i, R - 2) + 1)])
+    take(R - 1)
+    for i in range(R):
+        acc[i, 0:NO] += products(i, [R - 1] if i < R - 1 else [R - 1, 3 * R - 1])
 
     def deliver(i, d):
         dst = land.at[i, :, quarter]
@@ -177,9 +196,33 @@
     trace_values = jnp.zeros((QB, B), jnp.float32)
     trace_square = jnp.zeros((QB, B), jnp.float32)
     for i in range(R):
-        acc[i, 0:NO] += products(i, [*range(i, R), *range(2 * R, 2 * R + i + 1)])
         trace_values += L[i, 0, quarter].astype(jnp.float32)
         trace_square += acc[i, BAND]
+
+    def total(tile):
+        return jnp.sum(jnp.where(diagonal, tile, 0.0), axis=0, keepdims=True)
+
+    tx[fib] = jnp.where(rows == 0, total(trace_values), jnp.where(rows == 1, total(trace_square), 0.0))
+
+    def spread(buf, me, size, ssem, rsem, device):
+        return [remote(buf.at[me], buf.at[me], ssem.at[d - 1], rsem.at[d - 1], device(d)) for d in range(1, size)]
+
+    def add(buf, size):
+        tile = buf[0]
+        for k in range(1, size):
+            tile += buf[k]
+        return tile
+
+    def finish(i):
+        for d in range(1, n_fib):
+            deliver(i, d).wait_recv()
+        for t in range(T):
+            out_ref[i, t] = land[i, t].T
+
+    stage_x = spread(tx, fib, n_fib, tx_s, tx_r, along_fib)
+    stage_z = spread(tz, col, n_col, tz_s, tz_r, along_col)
+    stage_y = spread(ty, row, n_row, ty_s, ty_r, along_row)
+    for i in range(R):
         for d in range(n_fib):
             owner = lax.rem(fib + d, n_fib)
             for t in range(T):
@@ -188,49 +231,27 @@
                     land[i, t, quarter] = block
                 else:
                     send[d - 1, i, t] = block
-        if i >= 1:
+        if i == 0:
+            for copy in stage_x:
+                copy.start()
+        else:
             for d in range(1, n_fib):
                 deliver(i - 1, d).start()
-
-    def total(tile):
-        return jnp.sum(jnp.where(diagonal, tile, 0.0), axis=0, keepdims=True)
-
-    first = jnp.where(rows == 0, total(trace_values), jnp.where(rows == 1, total(trace_square), 0.0))
-    tx[fib] = first
     for d in range(1, n_fib):
         deliver(R - 1, d).start()
-
-    def spread(buf, me, size, ssem, rsem, device):
-        return [remote(buf.at[me], buf.at[me], ssem.at[d - 1], rsem.at[d - 1], device(d)) for d in range(1, size)]
-
-    def add(buf, size):
-        tile = buf[0]
-        for k in range(1, size):
-            tile += buf[k]
-        return tile
-
-    def finish(i):
-        for d in range(1, n_fib):
-            deliver(i, d).wait_recv()
-        for t in range(T):
-            out_ref[i, t] = land[i, t].T
-
-    stage_x = spread(tx, fib, n_fib, tx_s, tx_r, along_fib)
-    stage_z = spread(tz, col, n_col, tz_s, tz_r, along_col)
-    stage_y = spread(ty, row, n_row, ty_s, ty_r, along_row)
-    for copy in stage_x:
-        copy.start()
     for copy in stage_x:
         copy.wait_recv()
     tz[col] = add(tx, n_fib)
     for copy in stage_z:
         copy.start()
+    for i in range(2):
+        finish(i)
     for copy in stage_z:
         copy.wait_recv()
     ty[row] = add(tz, n_col)
     for copy in stage_y:
         copy.start()
-    for i in range(R):
+    for i in range(2, R):
         finish(i)
     for copy in stage_y:
         copy.wait_recv()
@@ -244,7 +265,8 @@
         for way in range(2):
             own(r, way).wait_send()
             relay(r, way).wait_send()
-            shift(r, way).wait_send()
+            for d in range(n_fib):
+                shift(r, way, d).wait_send()
         for d in range(1, n_fib):
             deliver(r, d).wait_send()
 
@@ -259,9 +281,11 @@
         return pl.pallas_call(
             functools.partial(kernel, sizes),
             out_shape=(jax.ShapeDtypeStruct((R, T, B, B), bf16), jax.ShapeDtypeStruct((2,), f32)),
-            in_specs=[vmem, vmem, smem],
+            in_specs=[pl.BlockSpec(memory_space=pl.ANY), vmem, smem],
             out_specs=(vmem, smem),
             scratch_shapes=[
+                pltpu.VMEM((R, T, B, B), bf16),
+                dma((R,)),
                 pltpu.VMEM((R, S + 1, B, B), bf16),
                 pltpu.VMEM((3 * R, NO + 2 * BAND, QB, B), bf16),
                 pltpu.VMEM((R, NO + 1, QB, B), f32),
@@ -273,7 +297,9 @@
                 pltpu.SMEM((16, B), i32),
                 pltpu.SMEM((8, B), i32),
                 pltpu.SMEM((8, B), i32),
-                *[dma((2, R))] * 6,
+                *[dma((2, R))] * 4,
+                dma((2, R, sizes[2])),
+                dma((2, R, sizes[2])),
                 dma((2,)),
                 dma((2,)),
                 dma((3,)),

time: 67.7 us -> 63.9 us (0.944)
  Pallas kernels: 64.5 us -> 60.6 us
    pallas_call x1, Pallas kernels: 64.5 us -> 60.6 us  [body(): pl.pallas_call(functools.partial(kernel, sizes), out_shape=(jax.ShapeDtyp...]
where the time goes in v2:
time: 63.9 us; the launch traced here: 63.7 us
  Pallas kernels  60.6 us (95%)
  local copies, waits for them, and re-layouts  2.45 us (4%)
  between operations  0.65 us (1%)
    pallas_call x1, Pallas kernels, body(): pl.pallas_call(functools.partial(kernel, sizes), out_shape=(jax.ShapeDtyp...  60.6 us
    unnamed x4, local copies, waits for them, and re-layouts  2.45 us

profile of v2, /device:TPU:1, one launch (start us, length us, event | category | flops | bytes accessed | tf_op | source)
XLA Modules:
  0.0 63.7 jit_solution(10473048118907881878)
XLA Ops:
  0.6 60.6 %shard_map.50 = (bf16[6,3,128,128]{3,2,1,0:T(8,128)(2,1)}, f32[2]{0:T(128)}) custom-call(bf16[6,3,128,128]{3,2,1,0:T(8,128)(2,1)} %v_ref.1, s32[6,12]{1,0:T(8,128)} %col_ref.1, s32[6]{0:T(128)} %cnt_ref.1), custom_call_target="tpu_custom_call" | custom-call | tf_op jit(solution)/shard_map/pallas_call | solution.py:281
  61.2 0.0 copy-start
  61.2 1.9 %copy.7 = bf16[6,3,128,128]{3,2,1,0:T(8,128)(2,1)} copy(bf16[6,3,128,128]{3,2,1,0:T(8,128)(2,1)} %get-tuple-element.4) | data formatting | bytes 1179648
  63.2 0.0 copy-done
  63.2 0.5 copy.8
Async XLA Ops:
  61.2 1.9 %copy-start = (f32[2]{0:T(128)S(1)}, f32[2]{0:T(128)}, u32[]{:S(2)}) copy-start(f32[2]{0:T(128)} %get-tuple-element.5) | copy-start | bytes 28

commit v3 on v2

--- a/solution.py
+++ b/solution.py
@@ -17,9 +17,8 @@
 QB = 32
 
 
-def kernel(sizes, v_ref, col_ref, cnt_ref, out_ref, tr_ref, held, held_s, L, Q, acc, send, land, tab, ntab, tx, tz, ty,
-           stab, sprev, snext, own_s, own_r, rel_s, rel_r, z_s, z_r, tab_s, tab_r, loc, out_s, out_r,
-           tx_s, tx_r, tz_s, tz_r, ty_s, ty_r, *halo):
+def kernel(sizes, v_ref, col_ref, cnt_ref, land, ty, held, col_v, cnt_v, L, Q, acc, send, tab, ntab, tx, tz,
+           stab, sprev, snext, held_s, loc, own_r, rel_r, z_r, out_r, once, *halo):
     n_row, n_col, n_fib = sizes
     n_blocks = n_row * n_col * R
     row, col, fib = (lax.axis_index(a) for a in ("row", "col", "fib"))
@@ -53,8 +52,13 @@
     quarter = pl.ds(mine, QB)
     prev, nxt = halo[:R], halo[R:]
 
+    (own_s, rel_s, z_s, tab_s, tab_r, out_s, tx_s, tx_r, tz_s, tz_r, ty_s, ty_r) = (once.at[k] for k in range(12))
+    whole = [
+        pltpu.make_async_copy(col_ref, col_v, loc.at[0]),
+        pltpu.make_async_copy(cnt_ref, cnt_v, loc.at[1]),
+    ]
     fetches = [pltpu.make_async_copy(v_ref.at[r], held.at[r], held_s.at[r]) for r in range(R)]
-    for fetch in fetches:
+    for fetch in fetches + whole:
         fetch.start()
 
     def flip(r):
@@ -64,25 +68,28 @@
 
     def own(r, way):
         part = L.at[r, pl.ds(T * fib, T)]
-        return remote(part, part, own_s.at[way, r], own_r.at[way, r], along_fib(1 - 2 * way))
+        return remote(part, part, own_s, own_r.at[r], along_fib(1 - 2 * way))
 
     def relay(r, way):
         cut = 2 - r % 2
         source = lax.rem(fib + (n_fib - 1 if way == 0 else 1), n_fib)
         part = L.at[r, pl.ds(T * source, cut)] if way == 0 else L.at[r, pl.ds(T * source + cut, T - cut)]
-        return remote(part, part, rel_s.at[way, r], rel_r.at[way, r], along_fib(1 - 2 * way))
+        return remote(part, part, rel_s, rel_r.at[r], along_fib(1 - 2 * way))
 
     def shift(r, way, d):
         part = pl.ds(T * lax.rem(fib + d, n_fib), T)
         dst = (prev if way == 0 else nxt)[r].at[part]
-        return remote(L.at[r, part, quarter], dst, z_s.at[way, r, d], z_r.at[way, r, d], along_group(1 - 2 * way))
+        return remote(L.at[r, part, quarter], dst, z_s, z_r.at[r // (R - 1)], along_group(1 - 2 * way))
+
+    def drain(ref, sem):
+        pltpu.make_async_copy(ref, ref, sem).wait()
 
     def both(make, *where):
         make(*where[:1], 0, *where[1:]).start()
         make(*where[:1], 1, *where[1:]).start()
 
     def tables(way):
-        return remote(tab.at[0:8], ntab.at[way], tab_s.at[way], tab_r.at[way], along_group(1 - 2 * way))
+        return remote(tab.at[0:8], ntab.at[way], tab_s, tab_r, along_group(1 - 2 * way))
 
     flip(0)
     flip(1)
@@ -92,13 +99,15 @@
     for r in range(2, R):
         flip(r)
 
+    for copy in whole:
+        copy.wait()
     rows = lax.broadcasted_iota(jnp.int32, (8, B), 0)
     lanes = lax.broadcasted_iota(jnp.int32, (8, B), 1)
     table, place = jnp.full((8, B), S, jnp.int32), jnp.full((8, B), NO, jnp.int32)
-    columns = jnp.concatenate([col_ref[...], jnp.zeros((8 - R, S), jnp.int32)], axis=0)
+    columns = jnp.concatenate([col_v[...], jnp.zeros((8 - R, S), jnp.int32)], axis=0)
     counts = jnp.zeros((8, B), jnp.int32)
     for r in range(R):
-        counts = jnp.where(rows == r, cnt_ref[r], counts)
+        counts = jnp.where(rows == r, cnt_v[r], counts)
     for s in range(S):
         offset = columns[:, s : s + 1] - (group * R + rows) + BAND
         offset = jnp.where(offset < 0, offset + n_blocks, offset)
@@ -120,32 +129,28 @@
         acc[r, NO] = jnp.zeros((QB, B), jnp.float32)
         L[r, S] = jnp.zeros((B, B), jnp.bfloat16)
 
-    local = pltpu.make_async_copy(tab, stab, loc.at[0])
+    local = pltpu.make_async_copy(tab, stab, loc.at[2])
     local.start()
     for r in range(R):
         both(shift, r, 0)
     tables(0).start()
     tables(1).start()
     for r in range(R):
-        own(r, 0).wait_recv()
-        own(r, 1).wait_recv()
+        drain(L.at[r, 0 : 2 * T], own_r.at[r])
         both(relay, r)
         if r + 2 < R:
             both(own, r + 2)
         both(shift, r, 1)
         both(shift, r, n_fib - 1)
         if r >= 1:
-            relay(r - 1, 0).wait_recv()
-            relay(r - 1, 1).wait_recv()
+            drain(L.at[r, 0:T], rel_r.at[r - 1])
             both(shift, r - 1, 2)
-    relay(R - 1, 0).wait_recv()
-    relay(R - 1, 1).wait_recv()
+    drain(L.at[0, 0:T], rel_r.at[R - 1])
     both(shift, R - 1, 2)
 
     local.wait()
-    tables(0).wait_recv()
-    tables(1).wait_recv()
-    near = (pltpu.make_async_copy(ntab.at[0], sprev, loc.at[1]), pltpu.make_async_copy(ntab.at[1], snext, loc.at[2]))
+    drain(ntab, tab_r)
+    near = (pltpu.make_async_copy(ntab.at[0], sprev, loc.at[0]), pltpu.make_async_copy(ntab.at[1], snext, loc.at[1]))
     for copy in near:
         copy.start()
 
@@ -173,24 +178,23 @@
     for copy in near:
         copy.wait()
     def take(r):
-        for way in range(2):
-            for d in range(n_fib):
-                shift(r, way, d).wait_recv()
         for o in range(NO):
             Q[r, BAND + o] = prev[r][sprev[r, o]]
             Q[2 * R + r, BAND + o] = nxt[r][snext[r, o]]
 
+    drain(L.at[0 : R - 1, 0 : S // 2], z_r.at[0])
     for r in range(R - 1):
         take(r)
     for i in range(R):
         acc[i, 0:NO] += products(i, [*range(i, R - 1), *range(2 * R, 2 * R + min(i, R - 2) + 1)])
+    drain(L.at[0, 0 : S // 2], z_r.at[1])
     take(R - 1)
     for i in range(R):
         acc[i, 0:NO] += products(i, [R - 1] if i < R - 1 else [R - 1, 3 * R - 1])
 
     def deliver(i, d):
         dst = land.at[i, :, quarter]
-        return remote(send.at[d - 1, i], dst, out_s.at[d - 1, i], out_r.at[d - 1, i], along_fib(d))
+        return remote(send.at[d - 1, i], dst, out_s, out_r.at[i], along_fib(d))
 
     diagonal = lax.broadcasted_iota(jnp.int32, (QB, B), 1) == lax.broadcasted_iota(jnp.int32, (QB, B), 0) + mine
     trace_values = jnp.zeros((QB, B), jnp.float32)
@@ -205,19 +209,13 @@
     tx[fib] = jnp.where(rows == 0, total(trace_values), jnp.where(rows == 1, total(trace_square), 0.0))
 
     def spread(buf, me, size, ssem, rsem, device):
-        return [remote(buf.at[me], buf.at[me], ssem.at[d - 1], rsem.at[d - 1], device(d)) for d in range(1, size)]
+        return [remote(buf.at[me], buf.at[me], ssem, rsem, device(d)) for d in range(1, size)]
 
     def add(buf, size):
         tile = buf[0]
         for k in range(1, size):
             tile += buf[k]
         return tile
-
-    def finish(i):
-        for d in range(1, n_fib):
-            deliver(i, d).wait_recv()
-        for t in range(T):
-            out_ref[i, t] = land[i, t].T
 
     stage_x = spread(tx, fib, n_fib, tx_s, tx_r, along_fib)
     stage_z = spread(tz, col, n_col, tz_s, tz_r, along_col)
@@ -239,36 +237,44 @@
                 deliver(i - 1, d).start()
     for d in range(1, n_fib):
         deliver(R - 1, d).start()
-    for copy in stage_x:
-        copy.wait_recv()
+    drain(tx.at[1:n_fib], tx_r)
     tz[col] = add(tx, n_fib)
     for copy in stage_z:
         copy.start()
-    for i in range(2):
-        finish(i)
-    for copy in stage_z:
-        copy.wait_recv()
+    drain(tz.at[1:n_col], tz_r)
     ty[row] = add(tz, n_col)
     for copy in stage_y:
         copy.start()
-    for i in range(2, R):
-        finish(i)
-    for copy in stage_y:
-        copy.wait_recv()
-    sums = add(ty, n_row)
+
+    drain(L.at[0:R, 0 : 2 * T], own_s)
+    drain(L.at[0:R, 0:T], rel_s)
+    drain(L.at[0:R, 0 : S // 2], z_s)
+    drain(tab, tab_s)
+    drain(send, out_s)
+    drain(tx.at[1:n_fib], tx_s)
+    drain(tz.at[1:n_col], tz_s)
+    for i in range(R):
+        drain(land.at[i, :, 0 : B - QB], out_r.at[i])
+    drain(ty.at[1:n_row], ty_r)
+    drain(ty.at[1:n_row], ty_s)
+
+
+def finish(land, ty, out_ref, tr_ref, out_v, sem):
+    copies = []
+    for i in range(R):
+        for t in range(T):
+            out_v[i, t] = land[i, t].T
+        copies.append(pltpu.make_async_copy(out_v.at[i], out_ref.at[i], sem.at[i]))
+        if i:
+            copies[i - 1].start()
+    copies[R - 1].start()
+    sums = ty[0]
+    for k in range(1, ty.shape[0]):
+        sums += ty[k]
     tr_ref[0] = jnp.sum(sums[0:1])
     tr_ref[1] = jnp.sum(sums[1:2])
-
-    for copy in [*stage_x, *stage_y, *stage_z, tables(0), tables(1)]:
-        copy.wait_send()
-    for r in range(R):
-        for way in range(2):
-            own(r, way).wait_send()
-            relay(r, way).wait_send()
-            for d in range(n_fib):
-                shift(r, way, d).wait_send()
-        for d in range(1, n_fib):
-            deliver(r, d).wait_send()
+    for copy in copies:
+        copy.wait()
 
 
 def solution(mesh):
@@ -278,38 +284,45 @@
 
     def body(values, columns, counts):
         vmem, smem = pl.BlockSpec(memory_space=pltpu.VMEM), pl.BlockSpec(memory_space=pltpu.SMEM)
-        return pl.pallas_call(
+        hbm = pl.BlockSpec(memory_space=pl.ANY)
+        land, ty = pl.pallas_call(
             functools.partial(kernel, sizes),
-            out_shape=(jax.ShapeDtypeStruct((R, T, B, B), bf16), jax.ShapeDtypeStruct((2,), f32)),
-            in_specs=[pl.BlockSpec(memory_space=pl.ANY), vmem, smem],
-            out_specs=(vmem, smem),
+            out_shape=(pltpu.VMEM((R, T, B, B), bf16), pltpu.VMEM((sizes[0], 8, B), f32)),
+            in_specs=[hbm, hbm, hbm],
+            out_specs=(vmem, vmem),
             scratch_shapes=[
                 pltpu.VMEM((R, T, B, B), bf16),
-                dma((R,)),
+                pltpu.VMEM((R, S), i32),
+                pltpu.SMEM((R,), i32),
                 pltpu.VMEM((R, S + 1, B, B), bf16),
                 pltpu.VMEM((3 * R, NO + 2 * BAND, QB, B), bf16),
                 pltpu.VMEM((R, NO + 1, QB, B), f32),
                 pltpu.VMEM((3, R, T, QB, B), bf16),
-                pltpu.VMEM((R, T, B, B), bf16),
                 pltpu.VMEM((16, B), i32),
                 pltpu.VMEM((2, 8, B), i32),
-                *(pltpu.VMEM((n, 8, B), f32) for n in (sizes[2], sizes[1], sizes[0])),
+                pltpu.VMEM((sizes[2], 8, B), f32),
+                pltpu.VMEM((sizes[1], 8, B), f32),
                 pltpu.SMEM((16, B), i32),
                 pltpu.SMEM((8, B), i32),
                 pltpu.SMEM((8, B), i32),
-                *[dma((2, R))] * 4,
-                dma((2, R, sizes[2])),
-                dma((2, R, sizes[2])),
+                dma((R,)),
+                dma((3,)),
+                dma((R,)),
+                dma((R,)),
                 dma((2,)),
-                dma((2,)),
-                dma((3,)),
-                dma((3, R)),
-                dma((3, R)),
-                *(dma((n - 1,)) for n in (sizes[2], sizes[2], sizes[1], sizes[1], sizes[0], sizes[0])),
+                dma((R,)),
+                dma((12,)),
                 *[pltpu.VMEM((S + 1, QB, B), bf16)] * (2 * R),
             ],
             compiler_params=pltpu.CompilerParams(collective_id=0, has_side_effects=True),
         )(values, columns, counts)
+        return pl.pallas_call(
+            finish,
+            out_shape=(jax.ShapeDtypeStruct((R, T, B, B), bf16), jax.ShapeDtypeStruct((2,), f32)),
+            in_specs=[vmem, vmem],
+            out_specs=(hbm, smem),
+            scratch_shapes=[pltpu.VMEM((R, T, B, B), bf16), dma((R,))],
+        )(*(pltpu.with_memory_space_constraint(a, pltpu.VMEM) for a in (land, ty)))
 
     in_specs = (P(("row", "col"), "fib", None, None), P(("row", "col"), None), P(("row", "col")))
     out_specs = (P(("row", "col"), "fib", None, None), P())

time: 63.9 us -> 59.2 us (0.926)
  local copies, waits for them, and re-layouts: 2.45 us -> 0 us
  Pallas kernels: 60.6 us -> 58.4 us
    unnamed x4 -> x0, local copies, waits for them, and re-layouts: 2.45 us -> none
    pallas_call x1 -> x2, Pallas kernels: 60.6 us -> 58.4 us  [the longest x1 56.9 us: body(): pl.pallas_call(functools.partial(kernel, sizes), out_shape=(pltpu.VMEM((R...]
where the time goes in v3:
time: 59.2 us; the launch traced here: 59 us
  Pallas kernels  58.4 us (99%)
  between operations  0.64 us (1%)
    pallas_call x1, Pallas kernels, body(): pl.pallas_call(functools.partial(kernel, sizes), out_shape=(pltpu.VMEM((R...  56.9 us
    pallas_call x1, Pallas kernels, body(): pl.pallas_call(finish, out_shape=(jax.ShapeDtypeStruct((R, T, B, B), bf16...  1.53 us

profile of v3, /device:TPU:1, one launch (start us, length us, event | category | flops | bytes accessed | tf_op | source)
XLA Modules:
  0.0 59.0 jit_solution(15133559725306259006)
XLA Ops:
  0.6 56.9 %shard_map.50 = (bf16[6,3,128,128]{3,2,1,0:T(8,128)(2,1)S(1)}, f32[16,8,128]{2,1,0:T(8,128)S(1)}) custom-call(bf16[6,3,128,128]{3,2,1,0:T(8,128)(2,1)} %v_ref.1, s32[6,12]{1,0:T(8,128)} %col_ref.1, s32[6]{0:T(128)} %cnt_ref.1), custom_call_target="tpu_custom_call" | custom-call | tf_op jit(solution)/shard_map/pallas_call | solution.py:288
  57.5 1.5 %shard_map.51 = (bf16[6,3,128,128]{3,2,1,0:T(8,128)(2,1)}, f32[2]{0:T(128)}) custom-call(bf16[6,3,128,128]{3,2,1,0:T(8,128)(2,1)S(1)} %get-tuple-element.4.land, f32[16,8,128]{2,1,0:T(8,128)S(1)} %get-tuple-element.5.ty), custom_call_target="tpu_custom_call" | custom-call | tf_op jit(solution)/shard_map/pallas_call | solution.py:319

commit v4 on v3

--- a/solution.py
+++ b/solution.py
@@ -17,8 +17,8 @@
 QB = 32
 
 
-def kernel(sizes, v_ref, col_ref, cnt_ref, land, ty, held, col_v, cnt_v, L, Q, acc, send, tab, ntab, tx, tz,
-           stab, sprev, snext, held_s, loc, own_r, rel_r, z_r, out_r, once, *halo):
+def kernel(sizes, v_ref, col_ref, cnt_ref, land, ty, held, col_v, cnt_v, E, Q, acc, send, tab, ntab, tx, tz,
+           stab, sprev, snext, held_s, loc, own_r, rel_r, z_r, out_r, once, known, *buffers):
     n_row, n_col, n_fib = sizes
     n_blocks = n_row * n_col * R
     row, col, fib = (lax.axis_index(a) for a in ("row", "col", "fib"))
@@ -37,8 +37,8 @@
         other = lax.rem(group + d + n_row * n_col, n_row * n_col)
         return (other // n_col, lax.rem(other, n_col), fib)
 
-    peers = [along_fib(d) for d in range(1, n_fib)] + [along_group(1), along_group(-1)]
-    peers += [along_col(d) for d in range(1, n_col)] + [along_row(d) for d in range(1, n_row)]
+    beside = [along_col(1), along_col(n_col - 1), *(along_row(d) for d in (1, 2, n_row - 2, n_row - 1))]
+    peers = [along_fib(d) for d in range(1, n_fib)] + [along_group(1), along_group(-1)] + beside
     barrier = pltpu.get_barrier_semaphore()
     for peer in peers:
         pl.semaphore_signal(barrier, inc=1, device_id=peer, device_id_type=MESH)
@@ -50,9 +50,12 @@
 
     mine = pl.multiple_of(fib * QB, QB)
     quarter = pl.ds(mine, QB)
+    L, halo = buffers[:R], buffers[R:]
     prev, nxt = halo[:R], halo[R:]
 
-    (own_s, rel_s, z_s, tab_s, tab_r, out_s, tx_s, tx_r, tz_s, tz_r, ty_s, ty_r) = (once.at[k] for k in range(12))
+    (own_s, rel_s, z_s, tab_s, tab_r, out_s, tx_s, tx_r, tz_s, tz_r, ty_s, ty_r, e_s, e_r) = (
+        once.at[k] for k in range(14)
+    )
     whole = [
         pltpu.make_async_copy(col_ref, col_v, loc.at[0]),
         pltpu.make_async_copy(cnt_ref, cnt_v, loc.at[1]),
@@ -64,22 +67,28 @@
     def flip(r):
         fetches[r].wait()
         for t in range(T):
-            L[r, T * fib + t] = held[r, t].T
+            L[r][T * fib + t] = held[r, t].T
 
     def own(r, way):
-        part = L.at[r, pl.ds(T * fib, T)]
+        part = L[r].at[pl.ds(T * fib, T)]
         return remote(part, part, own_s, own_r.at[r], along_fib(1 - 2 * way))
 
     def relay(r, way):
         cut = 2 - r % 2
         source = lax.rem(fib + (n_fib - 1 if way == 0 else 1), n_fib)
-        part = L.at[r, pl.ds(T * source, cut)] if way == 0 else L.at[r, pl.ds(T * source + cut, T - cut)]
+        part = L[r].at[pl.ds(T * source, cut)] if way == 0 else L[r].at[pl.ds(T * source + cut, T - cut)]
         return remote(part, part, rel_s, rel_r.at[r], along_fib(1 - 2 * way))
 
     def shift(r, way, d):
         part = pl.ds(T * lax.rem(fib + d, n_fib), T)
         dst = (prev if way == 0 else nxt)[r].at[part]
-        return remote(L.at[r, part, quarter], dst, z_s, z_r.at[r // (R - 1)], along_group(1 - 2 * way))
+        src = E.at[part] if r == R - 1 and d else L[r].at[part, quarter]
+        return remote(src, dst, z_s, z_r.at[r // (R - 2)], along_group(1 - 2 * way))
+
+    def early(d):
+        theirs = pl.ds(pl.multiple_of(lax.rem(fib + d, n_fib) * QB, QB), QB)
+        part = pl.ds(T * fib, T)
+        return remote(L[R - 1].at[part, theirs], E.at[part], e_s, e_r, along_fib(d))
 
     def drain(ref, sem):
         pltpu.make_async_copy(ref, ref, sem).wait()
@@ -98,6 +107,8 @@
     both(own, 1)
     for r in range(2, R):
         flip(r)
+    for d in range(1, n_fib):
+        early(d).start()
 
     for copy in whole:
         copy.wait()
@@ -127,7 +138,7 @@
         ref[S] = jnp.zeros((QB, B), jnp.bfloat16)
     for r in range(R):
         acc[r, NO] = jnp.zeros((QB, B), jnp.float32)
-        L[r, S] = jnp.zeros((B, B), jnp.bfloat16)
+        L[r][S] = jnp.zeros((B, B), jnp.bfloat16)
 
     local = pltpu.make_async_copy(tab, stab, loc.at[2])
     local.start()
@@ -135,34 +146,10 @@
         both(shift, r, 0)
     tables(0).start()
     tables(1).start()
-    for r in range(R):
-        drain(L.at[r, 0 : 2 * T], own_r.at[r])
-        both(relay, r)
-        if r + 2 < R:
-            both(own, r + 2)
-        both(shift, r, 1)
-        both(shift, r, n_fib - 1)
-        if r >= 1:
-            drain(L.at[r, 0:T], rel_r.at[r - 1])
-            both(shift, r - 1, 2)
-    drain(L.at[0, 0:T], rel_r.at[R - 1])
-    both(shift, R - 1, 2)
-
-    local.wait()
-    drain(ntab, tab_r)
     near = (pltpu.make_async_copy(ntab.at[0], sprev, loc.at[0]), pltpu.make_async_copy(ntab.at[1], snext, loc.at[1]))
-    for copy in near:
-        copy.start()
-
-    def place_own(r, _):
-        for o in range(NO):
-            Q[R + r, BAND + o] = L[r, stab[r, o], quarter]
-        return 0
-
-    lax.fori_loop(0, R, place_own, 0)
 
     def term(i, w):
-        return Q[w, pl.ds(BAND + R + i - w, NO)].reshape(NO * QB, B), L[i, stab[i, w - i]]
+        return Q[w, pl.ds(BAND + R + i - w, NO)].reshape(NO * QB, B), L[i][stab[i, w - i]]
 
     def products(i, window):
         pairs = [term(i, w) for w in window]
@@ -170,27 +157,62 @@
         left = jnp.concatenate([p[1] for p in pairs], axis=0)
         return jnp.dot(right, left, preferred_element_type=jnp.float32).reshape(NO, QB, B)
 
-    def own_part(i, _):
-        acc[i, 0:NO] = products(i, range(R, 2 * R))
-        return 0
-
-    lax.fori_loop(0, R, own_part, 0)
-    for copy in near:
-        copy.wait()
+    def within(r):
+        for o in range(NO):
+            Q[R + r, BAND + o] = L[r][stab[r, o], quarter]
+        acc[r, 0:NO] = products(r, range(R, R + r + 1))
+        for i in range(r):
+            acc[i, 0:NO] += products(i, [R + r])
+
     def take(r):
         for o in range(NO):
             Q[r, BAND + o] = prev[r][sprev[r, o]]
             Q[2 * R + r, BAND + o] = nxt[r][snext[r, o]]
 
-    drain(L.at[0 : R - 1, 0 : S // 2], z_r.at[0])
-    for r in range(R - 1):
+    def tell(k):
+        for peer in beside:
+            pl.semaphore_signal(known.at[k], inc=1, device_id=peer, device_id_type=MESH)
+
+    tell(0)
+    for r in range(R):
+        drain(L[r].at[0 : 2 * T], own_r.at[r])
+        both(relay, r)
+        if r + 2 < R:
+            both(own, r + 2)
+        if r < R - 1:
+            both(shift, r, 1)
+            both(shift, r, n_fib - 1)
+        if r == 1:
+            drain(E.at[0 : S - T], e_r)
+            for d in range(1, n_fib):
+                both(shift, R - 1, d)
+            local.wait()
+        if r >= 1:
+            drain(L[r].at[0:T], rel_r.at[r - 1])
+            both(shift, r - 1, 2)
+            within(r - 1)
+        if 2 <= r < 5:
+            pl.semaphore_wait(known.at[r - 2], len(beside))
+            if r < 4:
+                tell(r - 1)
+    drain(ntab, tab_r)
+    for copy in near:
+        copy.start()
+    drain(Q.at[0 : 2 * R, 0 : 2 * n_fib], z_r.at[0])
+    for copy in near:
+        copy.wait()
+    for r in range(R - 2):
         take(r)
-    for i in range(R):
-        acc[i, 0:NO] += products(i, [*range(i, R - 1), *range(2 * R, 2 * R + min(i, R - 2) + 1)])
-    drain(L.at[0, 0 : S // 2], z_r.at[1])
+    for i in range(R - 1):
+        acc[i, 0:NO] += products(i, [*range(i, R - 2), *range(2 * R, 2 * R + min(i, R - 3) + 1)])
+    drain(L[R - 1].at[0:T], rel_r.at[R - 1])
+    within(R - 1)
+    drain(Q.at[0:R, 0 : 2 * n_fib], z_r.at[1])
+    take(R - 2)
     take(R - 1)
     for i in range(R):
-        acc[i, 0:NO] += products(i, [R - 1] if i < R - 1 else [R - 1, 3 * R - 1])
+        late = [w for w in (R - 2, R - 1) if w >= i] + [2 * R + w for w in (R - 2, R - 1) if w <= i]
+        acc[i, 0:NO] += products(i, late if i < R - 1 else [R - 1, *range(2 * R, 3 * R)])
 
     def deliver(i, d):
         dst = land.at[i, :, quarter]
@@ -200,7 +222,7 @@
     trace_values = jnp.zeros((QB, B), jnp.float32)
     trace_square = jnp.zeros((QB, B), jnp.float32)
     for i in range(R):
-        trace_values += L[i, 0, quarter].astype(jnp.float32)
+        trace_values += L[i][0, quarter].astype(jnp.float32)
         trace_square += acc[i, BAND]
 
     def total(tile):
@@ -246,9 +268,10 @@
     for copy in stage_y:
         copy.start()
 
-    drain(L.at[0:R, 0 : 2 * T], own_s)
-    drain(L.at[0:R, 0:T], rel_s)
-    drain(L.at[0:R, 0 : S // 2], z_s)
+    drain(Q.at[:, 0 : 2 * n_fib], own_s)
+    drain(Q.at[:, 0:n_fib], rel_s)
+    drain(Q.at[:, 0 : 2 * n_fib], z_s)
+    drain(E.at[0 : S - T], e_s)
     drain(tab, tab_s)
     drain(send, out_s)
     drain(tx.at[1:n_fib], tx_s)
@@ -294,7 +317,7 @@
                 pltpu.VMEM((R, T, B, B), bf16),
                 pltpu.VMEM((R, S), i32),
                 pltpu.SMEM((R,), i32),
-                pltpu.VMEM((R, S + 1, B, B), bf16),
+                pltpu.VMEM((S, QB, B), bf16),
                 pltpu.VMEM((3 * R, NO + 2 * BAND, QB, B), bf16),
                 pltpu.VMEM((R, NO + 1, QB, B), f32),
                 pltpu.VMEM((3, R, T, QB, B), bf16),
@@ -311,7 +334,9 @@
                 dma((R,)),
                 dma((2,)),
                 dma((R,)),
-                dma((12,)),
+                dma((14,)),
+                pltpu.SemaphoreType.REGULAR((3,)),
+                *[pltpu.VMEM((S + 1, B, B), bf16)] * R,
                 *[pltpu.VMEM((S + 1, QB, B), bf16)] * (2 * R),
             ],
             compiler_params=pltpu.CompilerParams(collective_id=0, has_side_effects=True),

time: 59.2 us -> 55.3 us (0.934)
  Pallas kernels: 58.4 us -> 54.5 us
    pallas_call x1, Pallas kernels: 56.9 us -> 53 us  [body(): pl.pallas_call(functools.partial(kernel, sizes), out_shape=(pltpu.VMEM((R...]
where the time goes in v4:
time: 55.3 us; the launch traced here: 55.2 us
  Pallas kernels  54.5 us (99%)
  between operations  0.64 us (1%)
    pallas_call x1, Pallas kernels, body(): pl.pallas_call(functools.partial(kernel, sizes), out_shape=(pltpu.VMEM((R...  53 us
    pallas_call x1, Pallas kernels, body(): pl.pallas_call(finish, out_shape=(jax.ShapeDtypeStruct((R, T, B, B), bf16...  1.53 us

profile of v4, /device:TPU:1, one launch (start us, length us, event | category | flops | bytes accessed | tf_op | source)
XLA Modules:
  0.0 55.2 jit_solution(10211225096936317990)
XLA Ops:
  0.6 53.0 %shard_map.50 = (bf16[6,3,128,128]{3,2,1,0:T(8,128)(2,1)S(1)}, f32[16,8,128]{2,1,0:T(8,128)S(1)}) custom-call(bf16[6,3,128,128]{3,2,1,0:T(8,128)(2,1)} %v_ref.1, s32[6,12]{1,0:T(8,128)} %col_ref.1, s32[6]{0:T(128)} %cnt_ref.1), custom_call_target="tpu_custom_call" | custom-call | tf_op jit(solution)/shard_map/pallas_call | solution.py:311
  53.7 1.5 %shard_map.51 = (bf16[6,3,128,128]{3,2,1,0:T(8,128)(2,1)}, f32[2]{0:T(128)}) custom-call(bf16[6,3,128,128]{3,2,1,0:T(8,128)(2,1)S(1)} %get-tuple-element.4.land, f32[16,8,128]{2,1,0:T(8,128)S(1)} %get-tuple-element.5.ty), custom_call_target="tpu_custom_call" | custom-call | tf_op jit(solution)/shard_map/pallas_call | solution.py:344

commit v5 on v4

--- a/solution.py
+++ b/solution.py
@@ -38,7 +38,12 @@
         return (other // n_col, lax.rem(other, n_col), fib)
 
     beside = [along_col(1), along_col(n_col - 1), *(along_row(d) for d in (1, 2, n_row - 2, n_row - 1))]
-    peers = [along_fib(d) for d in range(1, n_fib)] + [along_group(1), along_group(-1)] + beside
+    core = lax.rem(row, 2)
+
+    def along_line(d):
+        return (row - core + lax.rem(core + d, 2), col, lax.rem(fib + d // 2, n_fib))
+
+    peers = [along_line(d) for d in range(1, 2 * n_fib)] + [along_fib(d) for d in range(1, n_fib)] + [along_group(1), along_group(-1)] + beside
     barrier = pltpu.get_barrier_semaphore()
     for peer in peers:
         pl.semaphore_signal(barrier, inc=1, device_id=peer, device_id_type=MESH)
@@ -105,8 +110,11 @@
     pl.semaphore_wait(barrier, len(peers))
     both(own, 0)
     both(own, 1)
-    for r in range(2, R):
-        flip(r)
+    flip(2)
+    flip(3)
+    both(own, 2)
+    flip(4)
+    flip(5)
     for d in range(1, n_fib):
         early(d).start()
 
@@ -177,8 +185,8 @@
     for r in range(R):
         drain(L[r].at[0 : 2 * T], own_r.at[r])
         both(relay, r)
-        if r + 2 < R:
-            both(own, r + 2)
+        if r + 3 < R:
+            both(own, r + 3)
         if r < R - 1:
             both(shift, r, 1)
             both(shift, r, n_fib - 1)
@@ -228,7 +236,8 @@
     def total(tile):
         return jnp.sum(jnp.where(diagonal, tile, 0.0), axis=0, keepdims=True)
 
-    tx[fib] = jnp.where(rows == 0, total(trace_values), jnp.where(rows == 1, total(trace_square), 0.0))
+    place_x = 2 * fib + core
+    tx[place_x] = jnp.where(rows == 0, total(trace_values), jnp.where(rows == 1, total(trace_square), 0.0))
 
     def spread(buf, me, size, ssem, rsem, device):
         return [remote(buf.at[me], buf.at[me], ssem, rsem, device(d)) for d in range(1, size)]
@@ -239,9 +248,9 @@
             tile += buf[k]
         return tile
 
-    stage_x = spread(tx, fib, n_fib, tx_s, tx_r, along_fib)
+    stage_x = spread(tx, place_x, 2 * n_fib, tx_s, tx_r, along_line)
     stage_z = spread(tz, col, n_col, tz_s, tz_r, along_col)
-    stage_y = spread(ty, row, n_row, ty_s, ty_r, along_row)
+    stage_y = spread(ty, row // 2, n_row // 2, ty_s, ty_r, lambda d: along_row(2 * d))
     for i in range(R):
         for d in range(n_fib):
             owner = lax.rem(fib + d, n_fib)
@@ -257,14 +266,15 @@
         else:
             for d in range(1, n_fib):
                 deliver(i - 1, d).start()
+        if i == R // 2:
+            drain(tx.at[1 : 2 * n_fib], tx_r)
+            tz[col] = add(tx, 2 * n_fib)
+            for copy in stage_z:
+                copy.start()
     for d in range(1, n_fib):
         deliver(R - 1, d).start()
-    drain(tx.at[1:n_fib], tx_r)
-    tz[col] = add(tx, n_fib)
-    for copy in stage_z:
-        copy.start()
     drain(tz.at[1:n_col], tz_r)
-    ty[row] = add(tz, n_col)
+    ty[row // 2] = add(tz, n_col)
     for copy in stage_y:
         copy.start()
 
@@ -274,12 +284,12 @@
     drain(E.at[0 : S - T], e_s)
     drain(tab, tab_s)
     drain(send, out_s)
-    drain(tx.at[1:n_fib], tx_s)
+    drain(tx.at[1 : 2 * n_fib], tx_s)
     drain(tz.at[1:n_col], tz_s)
     for i in range(R):
         drain(land.at[i, :, 0 : B - QB], out_r.at[i])
-    drain(ty.at[1:n_row], ty_r)
-    drain(ty.at[1:n_row], ty_s)
+    drain(ty.at[1 : n_row // 2], ty_r)
+    drain(ty.at[1 : n_row // 2], ty_s)
 
 
 def finish(land, ty, out_ref, tr_ref, out_v, sem):
@@ -310,7 +320,7 @@
         hbm = pl.BlockSpec(memory_space=pl.ANY)
         land, ty = pl.pallas_call(
             functools.partial(kernel, sizes),
-            out_shape=(pltpu.VMEM((R, T, B, B), bf16), pltpu.VMEM((sizes[0], 8, B), f32)),
+            out_shape=(pltpu.VMEM((R, T, B, B), bf16), pltpu.VMEM((sizes[0] // 2, 8, B), f32)),
             in_specs=[hbm, hbm, hbm],
             out_specs=(vmem, vmem),
             scratch_shapes=[
@@ -323,7 +333,7 @@
                 pltpu.VMEM((3, R, T, QB, B), bf16),
                 pltpu.VMEM((16, B), i32),
                 pltpu.VMEM((2, 8, B), i32),
-                pltpu.VMEM((sizes[2], 8, B), f32),
+                pltpu.VMEM((2 * sizes[2], 8, B), f32),
                 pltpu.VMEM((sizes[1], 8, B), f32),
                 pltpu.SMEM((16, B), i32),
                 pltpu.SMEM((8, B), i32),

time: 55.3 us -> 54.1 us (0.978)
  Pallas kernels: 54.5 us -> 53.3 us
    pallas_call x1, Pallas kernels: 53 us -> 51.8 us  [body(): pl.pallas_call(functools.partial(kernel, sizes), out_shape=(pltpu.VMEM((R...]
where the time goes in v5:
time: 54.1 us; the launch traced here: 54 us
  Pallas kernels  53.3 us (99%)
  between operations  0.64 us (1%)
    pallas_call x1, Pallas kernels, body(): pl.pallas_call(functools.partial(kernel, sizes), out_shape=(pltpu.VMEM((R...  51.8 us
    pallas_call x1, Pallas kernels, body(): pl.pallas_call(finish, out_shape=(jax.ShapeDtypeStruct((R, T, B, B), bf16...  1.52 us

profile of v5, /device:TPU:1, one launch (start us, length us, event | category | flops | bytes accessed | tf_op | source)
XLA Modules:
  0.0 54.0 jit_solution(3730040413377504640)
XLA Ops:
  0.6 51.8 %shard_map.50 = (bf16[6,3,128,128]{3,2,1,0:T(8,128)(2,1)S(1)}, f32[8,8,128]{2,1,0:T(8,128)S(1)}) custom-call(bf16[6,3,128,128]{3,2,1,0:T(8,128)(2,1)} %v_ref.1, s32[6,12]{1,0:T(8,128)} %col_ref.1, s32[6]{0:T(128)} %cnt_ref.1), custom_call_target="tpu_custom_call" | custom-call | tf_op jit(solution)/shard_map/pallas_call | solution.py:321
  52.5 1.5 %shard_map.51 = (bf16[6,3,128,128]{3,2,1,0:T(8,128)(2,1)}, f32[2]{0:T(128)}) custom-call(bf16[6,3,128,128]{3,2,1,0:T(8,128)(2,1)S(1)} %get-tuple-element.4.land, f32[8,8,128]{2,1,0:T(8,128)S(1)} %get-tuple-element.5.ty), custom_call_target="tpu_custom_call" | custom-call | tf_op jit(solution)/shard_map/pallas_call | solution.py:354

commit v6 on v5

--- a/solution.py
+++ b/solution.py
@@ -17,7 +17,7 @@
 QB = 32
 
 
-def kernel(sizes, v_ref, col_ref, cnt_ref, land, ty, held, col_v, cnt_v, E, Q, acc, send, tab, ntab, tx, tz,
+def kernel(sizes, v_ref, col_ref, cnt_ref, turned, ty, held, land, col_v, cnt_v, E, Q, acc, send, tab, ntab, tx, tz,
            stab, sprev, snext, held_s, loc, own_r, rel_r, z_r, out_r, once, known, *buffers):
     n_row, n_col, n_fib = sizes
     n_blocks = n_row * n_col * R
@@ -44,6 +44,9 @@
         return (row - core + lax.rem(core + d, 2), col, lax.rem(fib + d // 2, n_fib))
 
     peers = [along_line(d) for d in range(1, 2 * n_fib)] + [along_fib(d) for d in range(1, n_fib)] + [along_group(1), along_group(-1)] + beside
+    fetches = [pltpu.make_async_copy(v_ref.at[r], held.at[r], held_s.at[r]) for r in range(R)]
+    fetches[0].start()
+    fetches[1].start()
     barrier = pltpu.get_barrier_semaphore()
     for peer in peers:
         pl.semaphore_signal(barrier, inc=1, device_id=peer, device_id_type=MESH)
@@ -65,8 +68,7 @@
         pltpu.make_async_copy(col_ref, col_v, loc.at[0]),
         pltpu.make_async_copy(cnt_ref, cnt_v, loc.at[1]),
     ]
-    fetches = [pltpu.make_async_copy(v_ref.at[r], held.at[r], held_s.at[r]) for r in range(R)]
-    for fetch in fetches + whole:
+    for fetch in fetches[2:] + whole:
         fetch.start()
 
     def flip(r):
@@ -87,7 +89,7 @@
     def shift(r, way, d):
         part = pl.ds(T * lax.rem(fib + d, n_fib), T)
         dst = (prev if way == 0 else nxt)[r].at[part]
-        src = E.at[part] if r == R - 1 and d else L[r].at[part, quarter]
+        src = E.at[part] if r == R - 1 and d == 2 else L[r].at[part, quarter]
         return remote(src, dst, z_s, z_r.at[r // (R - 2)], along_group(1 - 2 * way))
 
     def early(d):
@@ -115,8 +117,7 @@
     both(own, 2)
     flip(4)
     flip(5)
-    for d in range(1, n_fib):
-        early(d).start()
+    early(2).start()
 
     for copy in whole:
         copy.wait()
@@ -187,13 +188,11 @@
         both(relay, r)
         if r + 3 < R:
             both(own, r + 3)
-        if r < R - 1:
-            both(shift, r, 1)
-            both(shift, r, n_fib - 1)
+        both(shift, r, 1)
+        both(shift, r, n_fib - 1)
         if r == 1:
-            drain(E.at[0 : S - T], e_r)
-            for d in range(1, n_fib):
-                both(shift, R - 1, d)
+            drain(E.at[0:T], e_r)
+            both(shift, R - 1, 2)
             local.wait()
         if r >= 1:
             drain(L[r].at[0:T], rel_r.at[r - 1])
@@ -281,26 +280,23 @@
     drain(Q.at[:, 0 : 2 * n_fib], own_s)
     drain(Q.at[:, 0:n_fib], rel_s)
     drain(Q.at[:, 0 : 2 * n_fib], z_s)
-    drain(E.at[0 : S - T], e_s)
+    drain(E.at[0:T], e_s)
     drain(tab, tab_s)
     drain(send, out_s)
     drain(tx.at[1 : 2 * n_fib], tx_s)
     drain(tz.at[1:n_col], tz_s)
     for i in range(R):
         drain(land.at[i, :, 0 : B - QB], out_r.at[i])
+        for t in range(T):
+            turned[i, t] = land[i, t].T
     drain(ty.at[1 : n_row // 2], ty_r)
     drain(ty.at[1 : n_row // 2], ty_s)
 
 
-def finish(land, ty, out_ref, tr_ref, out_v, sem):
-    copies = []
-    for i in range(R):
-        for t in range(T):
-            out_v[i, t] = land[i, t].T
-        copies.append(pltpu.make_async_copy(out_v.at[i], out_ref.at[i], sem.at[i]))
-        if i:
-            copies[i - 1].start()
-    copies[R - 1].start()
+def finish(turned, ty, out_ref, tr_ref, sem):
+    copies = [pltpu.make_async_copy(turned.at[i], out_ref.at[i], sem.at[i]) for i in range(R)]
+    for copy in copies:
+        copy.start()
     sums = ty[0]
     for k in range(1, ty.shape[0]):
         sums += ty[k]
@@ -318,12 +314,13 @@
     def body(values, columns, counts):
         vmem, smem = pl.BlockSpec(memory_space=pltpu.VMEM), pl.BlockSpec(memory_space=pltpu.SMEM)
         hbm = pl.BlockSpec(memory_space=pl.ANY)
-        land, ty = pl.pallas_call(
+        turned, ty = pl.pallas_call(
             functools.partial(kernel, sizes),
             out_shape=(pltpu.VMEM((R, T, B, B), bf16), pltpu.VMEM((sizes[0] // 2, 8, B), f32)),
             in_specs=[hbm, hbm, hbm],
             out_specs=(vmem, vmem),
             scratch_shapes=[
+                pltpu.VMEM((R, T, B, B), bf16),
                 pltpu.VMEM((R, T, B, B), bf16),
                 pltpu.VMEM((R, S), i32),
                 pltpu.SMEM((R,), i32),
@@ -356,8 +353,8 @@
             out_shape=(jax.ShapeDtypeStruct((R, T, B, B), bf16), jax.ShapeDtypeStruct((2,), f32)),
             in_specs=[vmem, vmem],
             out_specs=(hbm, smem),
-            scratch_shapes=[pltpu.VMEM((R, T, B, B), bf16), dma((R,))],
-        )(*(pltpu.with_memory_space_constraint(a, pltpu.VMEM) for a in (land, ty)))
+            scratch_shapes=[dma((R,))],
+        )(*(pltpu.with_memory_space_constraint(a, pltpu.VMEM) for a in (turned, ty)))
 
     in_specs = (P(("row", "col"), "fib", None, None), P(("row", "col"), None), P(("row", "col")))
     out_specs = (P(("row", "col"), "fib", None, None), P())

time: 54.1 us -> 53.5 us (0.989)
  Pallas kernels: 53.3 us -> 52.7 us
where the time goes in v6:
time: 53.5 us; the launch traced here: 53.3 us
  Pallas kernels  52.7 us (99%)
  between operations  0.64 us (1%)
    pallas_call x1, Pallas kernels, body(): pl.pallas_call(functools.partial(kernel, sizes), out_shape=(pltpu.VMEM((R...  51.3 us
    pallas_call x1, Pallas kernels, body(): pl.pallas_call(finish, out_shape=(jax.ShapeDtypeStruct((R, T, B, B), bf16...  1.37 us

profile of v6, /device:TPU:1, one launch (start us, length us, event | category | flops | bytes accessed | tf_op | source)
XLA Modules:
  0.0 53.3 jit_solution(13085028594825726424)
XLA Ops:
  0.6 51.3 %shard_map.50 = (bf16[6,3,128,128]{3,2,1,0:T(8,128)(2,1)S(1)}, f32[8,8,128]{2,1,0:T(8,128)S(1)}) custom-call(bf16[6,3,128,128]{3,2,1,0:T(8,128)(2,1)} %v_ref.1, s32[6,12]{1,0:T(8,128)} %col_ref.1, s32[6]{0:T(128)} %cnt_ref.1), custom_call_target="tpu_custom_call" | custom-call | tf_op jit(solution)/shard_map/pallas_call | solution.py:317
  51.9 1.4 %shard_map.51 = (bf16[6,3,128,128]{3,2,1,0:T(8,128)(2,1)}, f32[2]{0:T(128)}) custom-call(bf16[6,3,128,128]{3,2,1,0:T(8,128)(2,1)S(1)} %get-tuple-element.4.turned, f32[8,8,128]{2,1,0:T(8,128)S(1)} %get-tuple-element.5.ty), custom_call_target="tpu_custom_call" | custom-call | tf_op jit(solution)/shard_map/pallas_call | solution.py:351

commit v7 on v6

--- a/solution.py
+++ b/solution.py
@@ -43,7 +43,7 @@
     def along_line(d):
         return (row - core + lax.rem(core + d, 2), col, lax.rem(fib + d // 2, n_fib))
 
-    peers = [along_line(d) for d in range(1, 2 * n_fib)] + [along_fib(d) for d in range(1, n_fib)] + [along_group(1), along_group(-1)] + beside
+    peers = [along_line(d) for d in range(1, 2 * n_fib)] + [along_group(1), along_group(-1)] + beside
     fetches = [pltpu.make_async_copy(v_ref.at[r], held.at[r], held_s.at[r]) for r in range(R)]
     fetches[0].start()
     fetches[1].start()
@@ -190,6 +190,10 @@
             both(own, r + 3)
         both(shift, r, 1)
         both(shift, r, n_fib - 1)
+        if r == R - 1:
+            drain(ntab, tab_r)
+            for copy in near:
+                copy.start()
         if r == 1:
             drain(E.at[0:T], e_r)
             both(shift, R - 1, 2)
@@ -202,9 +206,6 @@
             pl.semaphore_wait(known.at[r - 2], len(beside))
             if r < 4:
                 tell(r - 1)
-    drain(ntab, tab_r)
-    for copy in near:
-        copy.start()
     drain(Q.at[0 : 2 * R, 0 : 2 * n_fib], z_r.at[0])
     for copy in near:
         copy.wait()

time: 53.5 us -> 53.5 us (level)
  no operation moved by 1% of the time
where the time goes in v7:
time: 53.5 us; the launch traced here: 53.3 us
  Pallas kernels  52.7 us (99%)
  between operations  0.64 us (1%)
    pallas_call x1, Pallas kernels, body(): pl.pallas_call(functools.partial(kernel, sizes), out_shape=(pltpu.VMEM((R...  51.3 us
    pallas_call x1, Pallas kernels, body(): pl.pallas_call(finish, out_shape=(jax.ShapeDtypeStruct((R, T, B, B), bf16...  1.37 us

profile of v7, /device:TPU:1, one launch (start us, length us, event | category | flops | bytes accessed | tf_op | source)
XLA Modules:
  0.0 53.3 jit_solution(2058941566272037558)
XLA Ops:
  0.6 51.3 %shard_map.50 = (bf16[6,3,128,128]{3,2,1,0:T(8,128)(2,1)S(1)}, f32[8,8,128]{2,1,0:T(8,128)S(1)}) custom-call(bf16[6,3,128,128]{3,2,1,0:T(8,128)(2,1)} %v_ref.1, s32[6,12]{1,0:T(8,128)} %col_ref.1, s32[6]{0:T(128)} %cnt_ref.1), custom_call_target="tpu_custom_call" | custom-call | tf_op jit(solution)/shard_map/pallas_call | solution.py:318
  51.9 1.4 %shard_map.51 = (bf16[6,3,128,128]{3,2,1,0:T(8,128)(2,1)}, f32[2]{0:T(128)}) custom-call(bf16[6,3,128,128]{3,2,1,0:T(8,128)(2,1)S(1)} %get-tuple-element.4.turned, f32[8,8,128]{2,1,0:T(8,128)S(1)} %get-tuple-element.5.ty), custom_call_target="tpu_custom_call" | custom-call | tf_op jit(solution)/shard_map/pallas_call | solution.py:352
